TPU v7x, 32 devices: a whole 2x2x4 slice. The times are simulated.
32 devices in a mesh: rows: 16 (over z, y, x), cols: 2 (over core).
Axes of the slice: x: 2, y: 2, z: 4, core: 2. Of those that a mesh axis runs over, the one named last changes fastest.
Arguments:
- points: bfloat16 [20480, 512], P('rows', 'cols'), may hold values from -6 to 6
- factor: bfloat16 [20480, 1024], P('rows', 'cols'), may hold values from -2 to 2
- weights: float32 [20480], P('rows'), may hold values from -4 to 4
- pivot_slots: int32 [4, 128], replicated, may hold values from 0 to 1279, as said below
- pivot_owners: int32 [4, 128], replicated, may hold values from 0 to 15
Outputs:
- new_panels: bfloat16 [20480, 512], P('rows', 'cols')
- gram_old: float32 [512, 1024], P('rows', 'cols')
- gram_new: float32 [512, 512], P('rows', 'cols')
Inputs may be any that keep to these rules, and one draw needn't show every extreme that they name: Pivot k of panel q is row pivot_slots[q,k] of the block of device pivot_owners[q,k]; the pivots of all panels together are distinct points.
All inputs are finite; a program needn't handle non-finite values.
Results may differ from a plain program's by a relative error of at most 0.009.
Values may be sent and summed in bfloat16 or wider, within the bound.
A program may use at most 64 MiB of HBM per device.

v0:
```python
import math
import jax
import jax.numpy as jnp
from jax import lax
from jax.sharding import PartitionSpec as P

F = 512
R = 1024
RIDGE_LEVEL = 1.0


def body(points, factor, weights, pivot_slots, pivot_owners):
    rows_here = points.shape[0]
    panel = pivot_slots.shape[1]
    panel_count = pivot_slots.shape[0]
    device = lax.axis_index("rows")
    column = lax.axis_index("cols")
    halves = lax.axis_size("cols")
    total_rows = rows_here * lax.axis_size("rows")
    identity = jnp.eye(panel, dtype=jnp.float32)
    half_rows = rows_here // halves
    full_points, full_factor = (
        lax.all_to_all(points, "cols", split_axis=0, concat_axis=1, tiled=True),
        lax.all_to_all(factor, "cols", split_axis=0, concat_axis=1, tiled=True),
    )
    local_ids = device * rows_here + column * half_rows + jnp.arange(half_rows, dtype=jnp.int32)
    local_norms = jnp.sum(jnp.square(full_points.astype(jnp.float32)), axis=1)
    built_half = jnp.zeros((half_rows, panel_count * panel), jnp.bfloat16)
    for index in range(panel_count):
        slots = pivot_slots[index]
        owners = pivot_owners[index]
        pivot_ids = owners * rows_here + slots
        chosen = ((owners == device) & (slots // half_rows == column))[:, None]
        local_slots = slots % half_rows
        sel_points = jnp.where(
            chosen, jnp.take(full_points, local_slots, axis=0).astype(jnp.float32), 0.0
        )
        sel_factor = jnp.where(
            chosen, jnp.take(full_factor, local_slots, axis=0).astype(jnp.float32), 0.0
        )
        sel_built = jnp.where(
            chosen, jnp.take(built_half, local_slots, axis=0).astype(jnp.float32), 0.0
        )
        sel_points, sel_factor, sel_built = lax.psum(
            (sel_points, sel_factor, sel_built), ("rows", "cols")
        )
        piv_norms = jnp.sum(jnp.square(sel_points), axis=1)
        piv_points = sel_points.astype(jnp.bfloat16)
        piv_factor = sel_factor.astype(jnp.bfloat16)
        piv_built = sel_built.astype(jnp.bfloat16)
        cross = jnp.dot(full_points, piv_points.T, preferred_element_type=jnp.float32)
        dist = local_norms[:, None] + piv_norms[None, :] - 2.0 * cross
        schur = jnp.dot(full_factor, piv_factor.T, preferred_element_type=jnp.float32)
        block_dist = (
            piv_norms[:, None]
            + piv_norms[None, :]
            - 2.0 * jnp.dot(piv_points, piv_points.T, preferred_element_type=jnp.float32)
        )
        block_schur = jnp.dot(piv_factor, piv_factor.T, preferred_element_type=jnp.float32)
        ridge = jnp.where(local_ids[:, None] == pivot_ids[None, :], RIDGE_LEVEL, 0.0)
        columns = (
            jnp.exp(-dist / F)
            + ridge
            + schur / (3.0 * R)
            - jnp.dot(built_half, piv_built.T, preferred_element_type=jnp.float32)
        )
        block = (
            jnp.exp(-block_dist / F)
            + RIDGE_LEVEL * identity
            + block_schur / (3.0 * R)
            - jnp.dot(piv_built, piv_built.T, preferred_element_type=jnp.float32)
        )
        lower = jnp.linalg.cholesky(block)
        inverse = lax.linalg.triangular_solve(lower, identity, left_side=True, lower=True)
        fresh = jnp.dot(columns, inverse.T, precision=lax.Precision.HIGHEST).astype(jnp.bfloat16)
        built_half = built_half.at[:, index * panel : (index + 1) * panel].set(fresh)
    built = lax.all_gather(built_half, "cols", axis=0, tiled=True)
    width = built.shape[1] // halves
    own_columns = lax.dynamic_slice_in_dim(built, column * width, width, 1)
    weighted = (built.astype(jnp.float32) * weights[:, None]).astype(jnp.bfloat16)
    dims = (((0,), (0,)), ((), ()))
    old_part = lax.dot_general(weighted, factor, dims, preferred_element_type=jnp.float32)
    new_part = lax.dot_general(weighted, own_columns, dims, preferred_element_type=jnp.float32)
    old_full, new_full = lax.psum((old_part, new_part), "rows")
    out_rows = old_part.shape[0] // lax.axis_size("rows")
    old_sum = lax.dynamic_slice_in_dim(old_full, device * out_rows, out_rows, 0)
    new_sum = lax.dynamic_slice_in_dim(new_full, device * out_rows, out_rows, 0)
    scale = panel / math.sqrt(total_rows)
    return (own_columns, old_sum * scale, new_sum * scale)


def solution(mesh):
    return jax.shard_map(
        body,
        mesh=mesh,
        in_specs=(P("rows", "cols"), P("rows", "cols"), P("rows"), P(), P()),
        out_specs=(P("rows", "cols"), P("rows", "cols"), P("rows", "cols")),
        check_vma=False,
    )
```

profile of v0, /device:TPU:0, one launch (start us, length us, event | category | flops | bytes accessed | tf_op | source)
XLA Modules:
  0.0 558.6 jit_solution(13490840416334126539)
XLA Ops:
  7.2 3.5 all-to-all-start
  11.4 1.1 all-to-all-done
  12.5 3.6 all-to-all-start.1
  18.6 1.5 gather_fusion
  20.2 1.6 gather_fusion.2
  23.4 1.5 convert_select_fusion.9
  24.9 1.0 convert_select_fusion.11
  27.5 1.1 copy-done.1
  28.6 1.5 copy.57
  30.1 1.7 gather_fusion.1
  31.8 1.6 gather_fusion.4
  33.4 1.7 gather_fusion.7
  35.1 1.1 gather_fusion.10
  36.2 1.1 convert_select_fusion.3
  37.3 1.9 convert_select_fusion.2
  39.3 1.9 convert_select_fusion.1
  41.2 1.0 convert_select_fusion
  42.1 50.2 %all-reduce.17 = (bf16[128,1024]{1,0:T(8,128)(2,1)S(1)}, bf16[128,512]{1,0:T(8,128)(2,1)S(1)}) all-reduce(f32[128,1024]{1,0:T(8,128)S(1)} %convert_select_fusion.3, f32[128,512]{1,0:T(8,128)} %get-tuple-element.94), channel_id=1, replica_groups=mesh['rows'=16,'cols'=2] {'rows','cols'}, use_global_device_ids=true, to_apply=%region_4.7 | all-reduce | flops 196608 | bytes 1179648 | tf_op jit(solution)/shard_map/psum | solution.py:44
  95.4 66.1 %all-reduce.14.cloned.1.call-done = (f32[128,512]{1,0:T(8,128)}, f32[128,512]{1,0:T(8,128)}, f32[128,512]{1,0:T(8,128)}, f32[128,512]{1,0:T(8,128)}) async-done(((f32[128,512]{1,0:T(8,128)}, f32[128,512]{1,0:T(8,128)}, f32[128,512]{1,0:T(8,128)}, f32[128,512]{1,0:T(8,128)}), (f32[128,512]{1,0:T(8,128)}, f32[128,512]{1,0:T(8,128)}, f32[128,512]{1,0:T(8,128)}, ...) | async-done | bytes 1048592 | tf_op jit(solution)/shard_map/psum | solution.py:44
  161.5 1.1 multiply_reduce_fusion.4
  162.6 1.2 fusion.43
  164.2 11.7 %cholesky.74 = f32[128,128]{1,0:T(8,128)S(1)} custom-call(f32[128,128]{1,0:T(8,128)S(1)} %fusion.93), custom_call_target="Cholesky" | custom-call | tf_op jit(solution)/shard_map/jit(cholesky)/cholesky | solution.py:73
  177.2 9.8 %custom-call.8 = f32[1,128,128]{1,2,0:T(8,128)S(1)} custom-call(f32[1,128,128]{2,1,0:T(8,128)S(1)} %fusion.82), custom_call_target="InvertDiagBlocksLowerTriangular" | custom-call | tf_op jit(solution)/shard_map/triangular_solve/custom-call.0 | solution.py:74
  188.1 1.1 fusion.33
  189.2 1.0 gather_fusion.5
  190.3 47.6 %all-reduce.18 = (bf16[128,1024]{1,0:T(8,128)(2,1)S(1)}, bf16[128,512]{1,0:T(8,128)(2,1)S(1)}) all-reduce(f32[128,1024]{1,0:T(8,128)} %convert_select_fusion.2, f32[128,512]{1,0:T(8,128)S(1)} %convert_select_fusion.8), channel_id=1, replica_groups=mesh['rows'=16,'cols'=2] {'rows','cols'}, use_global_device_ids=true, to_apply=%region_11.16 | all-reduce | flops 196608 | bytes 1179648 | tf_op jit(solution)/shard_map/psum | solution.py:44
  238.2 1.2 fusion.17
  240.1 11.7 %cholesky.85 = f32[128,128]{1,0:T(8,128)S(1)} custom-call(f32[128,128]{1,0:T(8,128)S(1)} %fusion.91), custom_call_target="Cholesky" | custom-call | tf_op jit(solution)/shard_map/jit(cholesky)/cholesky | solution.py:73
  253.1 9.8 %custom-call.9 = f32[1,128,128]{1,2,0:T(8,128)S(1)} custom-call(f32[1,128,128]{2,1,0:T(8,128)S(1)} %fusion.83), custom_call_target="InvertDiagBlocksLowerTriangular" | custom-call | tf_op jit(solution)/shard_map/triangular_solve/custom-call.0 | solution.py:74
  263.3 1.3 fusion.16
  264.9 1.1 fusion.35
  266.0 1.0 gather_fusion.8
  267.1 45.8 %all-reduce.19 = (bf16[128,1024]{1,0:T(8,128)(2,1)S(1)}, bf16[128,512]{1,0:T(8,128)(2,1)}) all-reduce(f32[128,1024]{1,0:T(8,128)} %convert_select_fusion.1, f32[128,512]{1,0:T(8,128)S(1)} %convert_select_fusion.6), channel_id=1, replica_groups=mesh['rows'=16,'cols'=2] {'rows','cols'}, use_global_device_ids=true, to_apply=%region_16.21 | all-reduce | flops 196608 | bytes 1179648 | tf_op jit(solution)/shard_map/psum | solution.py:44
  314.5 11.7 %cholesky.96 = f32[128,128]{1,0:T(8,128)S(1)} custom-call(f32[128,128]{1,0:T(8,128)S(1)} %fusion.89), custom_call_target="Cholesky" | custom-call | tf_op jit(solution)/shard_map/jit(cholesky)/cholesky | solution.py:73
  327.6 9.8 %custom-call.10 = f32[1,128,128]{1,2,0:T(8,128)S(1)} custom-call(f32[1,128,128]{2,1,0:T(8,128)S(1)} %fusion.84), custom_call_target="InvertDiagBlocksLowerTriangular" | custom-call | tf_op jit(solution)/shard_map/triangular_solve/custom-call.0 | solution.py:74
  337.7 1.0 fusion.23
  339.0 1.2 fusion.37
  340.2 1.0 gather_fusion.11
  341.3 47.0 %all-reduce.20 = (bf16[128,1024]{1,0:T(8,128)(2,1)S(1)}, bf16[128,512]{1,0:T(8,128)(2,1)}) all-reduce(f32[128,1024]{1,0:T(8,128)} %convert_select_fusion, f32[128,512]{1,0:T(8,128)S(1)} %convert_select_fusion.4), channel_id=1, replica_groups=mesh['rows'=16,'cols'=2] {'rows','cols'}, use_global_device_ids=true, to_apply=%region_20.25 | all-reduce | flops 196608 | bytes 1179648 | tf_op jit(solution)/shard_map/psum | solution.py:44
  389.9 11.7 %cholesky.107 = f32[128,128]{1,0:T(8,128)S(1)} custom-call(f32[128,128]{1,0:T(8,128)S(1)} %fusion.87), custom_call_target="Cholesky" | custom-call | tf_op jit(solution)/shard_map/jit(cholesky)/cholesky | solution.py:73
  403.0 9.8 %custom-call.11 = f32[1,128,128]{1,2,0:T(8,128)S(1)} custom-call(f32[1,128,128]{2,1,0:T(8,128)S(1)} %fusion.85), custom_call_target="InvertDiagBlocksLowerTriangular" | custom-call | tf_op jit(solution)/shard_map/triangular_solve/custom-call.0 | solution.py:74
  415.2 8.4 %all-gather.2.cloned.1.call-done = bf16[1280,512]{1,0:T(8,128)(2,1)} async-done(((bf16[640,512]{1,0:T(8,128)(2,1)}), bf16[1280,512]{1,0:T(8,128)(2,1)}) %all-gather.2.cloned.1.call-update) | async-done | bytes 1310736 | tf_op jit(solution)/shard_map/all_gather | solution.py:77
  423.6 1.1 constant_dynamic-slice_fusion
  424.8 3.5 fusion.63
  428.3 1.7 fusion.62
  430.0 119.0 %all-reduce.16.cloned.1.call-done = (f32[512,512]{1,0:T(8,128)}, f32[512,256]{1,0:T(8,128)}) async-done(((f32[512,512]{1,0:T(8,128)}, f32[512,256]{1,0:T(8,128)}), (f32[512,512]{1,0:T(8,128)}, f32[512,256]{1,0:T(8,128)})) %all-reduce.16.cloned.1.call-update) | async-done | bytes 1572880 | tf_op jit(solution)/shard_map/psum | solution.py:84
  549.0 1.5 dynamic-slice_multiply_fusion
  550.5 1.4 dynamic-slice_multiply_fusion.1
  (153 shorter events, 23.8 us)
Async XLA Ops:
  7.2 3.6 copy-start.25
  7.2 3.6 copy-start.23
  7.2 5.4 all-to-all-start
  11.4 27.9 %copy-start.17 = (pred[128]{0:T(512)(128)(4,1)}, pred[128]{0:T(512)(128)(4,1)S(1)}, u32[]{:S(2)}) copy-start(pred[128]{0:T(512)(128)(4,1)S(1)} %get-tuple-element.89) | copy-start | bytes 388
  11.4 29.8 %copy-start.15 = (pred[128]{0:T(512)(128)(4,1)}, pred[128]{0:T(512)(128)(4,1)S(1)}, u32[]{:S(2)}) copy-start(pred[128]{0:T(512)(128)(4,1)S(1)} %get-tuple-element.91) | copy-start | bytes 388
  11.4 4.9 copy-start.28
  12.5 15.0 %all-to-all-start.1 = ((bf16[2,640,512]{2,1,0:T(8,128)(2,1)}), bf16[2,640,512]{2,1,0:T(8,128)(2,1)S(1)}, u32[]{:S(2)}, u32[]{:S(2)}) async-start(bf16[2,640,512]{2,1,0:T(8,128)(2,1)} %bitcast.251), calls=%async_computation.1 | async-start | bytes 2621440 | tf_op jit(solution)/shard_map/all_to_all | solution.py:24
  16.2 145.3 %all-reduce.14.cloned.1.call-start = ((), (), s32[]{:S(2)}) async-start(), calls=%async_computation.3 | async-start | bytes 2097152 | tf_op jit(solution)/shard_map/psum | solution.py:44
  16.3 1.7 copy-start.27
  18.0 0.6 copy-start.30
  21.8 3.1 copy-start.12
  21.8 3.1 copy-start.13
  21.8 3.1 copy-start.31
  21.8 3.1 copy-start.33
  22.5 9.3 %copy-start.29 = (s32[1024]{0:T(1024)}, s32[1024]{0:T(1024)S(1)}, u32[]{:S(2)}) copy-start(s32[1024]{0:T(1024)S(1)} %pad_clamp_fusion.2) | copy-start | bytes 12292
  24.9 2.0 copy-start.24
  24.9 2.0 copy-start.26
  26.9 396.7 %all-gather.2.cloned.1.call-start = ((), (), s32[]{:S(2)}) async-start(), calls=%async_computation.2 | async-start | bytes 1966080 | tf_op jit(solution)/shard_map/all_gather | solution.py:77
  27.5 1.1 copy-start.1
  35.1 1.1 copy-start.32
  35.1 1.1 copy-start.34
  35.1 2.3 copy-start.19
  35.1 2.3 copy-start.21
  95.4 91.9 %copy-start.37 = (s32[128]{0:T(128)S(1)}, s32[128]{0:T(128)}, u32[]{:S(2)}) copy-start(s32[128]{0:T(128)} %get-tuple-element.78) | copy-start | bytes 1540
  161.5 25.9 %copy-start.5 = (f32[128,512]{1,0:T(8,128)S(1)}, f32[128,512]{1,0:T(8,128)}, u32[]{:S(2)}) copy-start(f32[128,512]{1,0:T(8,128)} %get-tuple-element.63) | copy-start | bytes 786436
  188.0 2.2 copy-start.20
  188.0 2.2 copy-start.22
  238.0 1.5 copy-start.4
  239.4 23.8 %copy-start.36 = (s32[128]{0:T(128)S(1)}, s32[128]{0:T(128)}, u32[]{:S(2)}) copy-start(s32[128]{0:T(128)} %get-tuple-element.79) | copy-start | bytes 1540
  264.6 2.4 copy-start.18
  312.9 0.9 copy-start.3
  313.1 1.0 copy-start.9
  314.2 24.5 %copy-start.10 = (bf16[128,512]{1,0:T(8,128)(2,1)S(1)}, bf16[128,512]{1,0:T(8,128)(2,1)}, u32[]{:S(2)}) copy-start(bf16[128,512]{1,0:T(8,128)(2,1)} %get-tuple-element.58) | copy-start | bytes 393220
  339.0 2.2 copy-start.16
  388.3 0.9 copy-start.2
  388.5 1.0 copy-start.7
  389.1 24.0 %copy-start.35 = (s32[128]{0:T(128)S(1)}, s32[128]{0:T(128)}, u32[]{:S(2)}) copy-start(s32[128]{0:T(128)} %get-tuple-element.77) | copy-start | bytes 1540
  389.6 23.9 %copy-start.8 = (bf16[128,512]{1,0:T(8,128)(2,1)S(1)}, bf16[128,512]{1,0:T(8,128)(2,1)}, u32[]{:S(2)}) copy-start(bf16[128,512]{1,0:T(8,128)(2,1)} %get-tuple-element.56) | copy-start | bytes 393220
  413.8 10.9 %copy-start.6 = (bf16[1280,512]{1,0:T(8,128)(2,1)S(1)}, bf16[1280,512]{1,0:T(8,128)(2,1)}, u32[]{:S(2)}) copy-start(bf16[1280,512]{1,0:T(8,128)(2,1)} %param.21) | copy-start | bytes 3932164
  413.8 10.9 %copy-start.38 = (f32[1280]{0:T(1024)S(1)}, f32[1280]{0:T(1024)}, u32[]{:S(2)}) copy-start(f32[1280]{0:T(1024)} %param.22) | copy-start | bytes 15364
  414.3 0.8 copy-start
  415.1 133.8 %all-reduce.16.cloned.1.call-start = ((), (), s32[]{:S(2)}) async-start(), calls=%async_computation.4 | async-start | bytes 3145728 | tf_op jit(solution)/shard_map/psum | solution.py:84
  424.7 3.6 copy-start.11
  424.7 3.6 copy-start.14
Sparse Core Ops, SparseCore 0:
  27.0 134.4 all-reduce.13
  415.3 8.2 all-gather.1
  430.1 118.8 all-reduce.15
where the time goes:
time: 563 us; the launch traced here: 559 us
  waiting for transfers between devices  195 us (35%)
  blocking collectives  191 us (34%)
  other arithmetic  110 us (20%)
  local copies, waits for them, and re-layouts  20.8 us (4%)
  matrix products  20.8 us (4%)
  between operations  14.9 us (3%)
  starting transfers between devices  7.27 us (1%)
    psum x4, blocking collectives, body(): lax.psum((sel_points, sel_factor, sel_built), ('rows', 'cols'))  191 us
    psum x1, waiting for transfers between devices, body(): old_full, new_full = lax.psum((old_part, new_part), 'rows')  119 us
    psum x1, waiting for transfers between devices, body(): lax.psum((sel_points, sel_factor, sel_built), ('rows', 'cols'))  66.1 us
    another operation x12, other arithmetic, body(): lower = jnp.linalg.cholesky(block)  49.6 us
    another operation x8, other arithmetic, body(): lax.linalg.triangular_solve(lower, identity, left_side=True, lower=True)  41.9 us
  transfers between devices with their start and end apart: 5, of which 4 were waited for; matrix products, arithmetic and copies ran while one was open for 5% of the time, Pallas kernels for 0%

commit v1 on v0

--- a/solution.py
+++ b/solution.py
@@ -42,7 +42,7 @@
             chosen, jnp.take(built_half, local_slots, axis=0).astype(jnp.float32), 0.0
         )
         sel_points, sel_factor, sel_built = lax.psum(
-            (sel_points, sel_factor, sel_built), ("rows", "cols")
+            lax.psum((sel_points, sel_factor, sel_built), "cols"), "rows"
         )
         piv_norms = jnp.sum(jnp.square(sel_points), axis=1)
         piv_points = sel_points.astype(jnp.bfloat16)

time: 563 us -> 759 us (1.35)
  blocking collectives: 191 us -> 351 us
  waiting for transfers between devices: 195 us -> 223 us
  other arithmetic: 110 us -> 118 us
    psum x4, blocking collectives: 191 us -> 351 us  [body(): lax.psum(lax.psum((sel_points, sel_factor, sel_built), 'cols'), 'rows')]
    psum x1 -> x5, waiting for transfers between devices: 66.1 us -> 97 us  [the longest x4 65.2 us: body(): lax.psum((sel_points, sel_factor, sel_built), 'cols')]
  transfers between devices with their start and end apart: 5 -> 9, of which waited for: 4 -> 8; matrix products, arithmetic and copies ran while one was open for 5% -> 2% of each run, Pallas kernels for 0% -> 0%
where the time goes in v1:
time: 759 us; the launch traced here: 754 us
  blocking collectives  351 us (46%)
  waiting for transfers between devices  223 us (29%)
  other arithmetic  118 us (16%)
  matrix products  20.5 us (3%)
  local copies, waits for them, and re-layouts  19.3 us (3%)
  between operations  15.1 us (2%)
    psum x4, blocking collectives, body(): lax.psum(lax.psum((sel_points, sel_factor, sel_built), 'cols'), 'rows')  351 us
    psum x1, waiting for transfers between devices, body(): old_full, new_full = lax.psum((old_part, new_part), 'rows')  119 us
    psum x4, waiting for transfers between devices, body(): lax.psum((sel_points, sel_factor, sel_built), 'cols')  65.2 us
    another operation x12, other arithmetic, body(): lower = jnp.linalg.cholesky(block)  52.7 us
    another operation x8, other arithmetic, body(): lax.linalg.triangular_solve(lower, identity, left_side=True, lower=True)  44.8 us
    psum x1, waiting for transfers between devices, body(): lax.psum(lax.psum((sel_points, sel_factor, sel_built), 'cols'), 'rows')  31.8 us
  transfers between devices with their start and end apart: 9, of which 8 were waited for; matrix products, arithmetic and copies ran while one was open for 2% of the time, Pallas kernels for 0%

profile of v1, /device:TPU:0, one launch (start us, length us, event | category | flops | bytes accessed | tf_op | source)
XLA Modules:
  0.0 753.7 jit_solution(13155407943061798179)
XLA Ops:
  7.2 3.5 all-to-all-start
  11.4 1.1 all-to-all-done
  12.5 3.6 all-to-all-start.1
  18.1 1.6 gather_fusion.2
  22.8 1.1 copy-done.1
  23.8 1.5 copy.57
  25.4 1.1 gather_fusion.1
  26.5 1.6 convert_select_fusion.3
  28.0 1.7 convert_select_fusion.11
  30.9 1.0 gather_fusion.4
  33.1 21.9 %all-reduce.32.cloned.1.call-done = (f32[128,1024]{1,0:T(8,128)}, f32[128,512]{1,0:T(8,128)}, f32[128,512]{1,0:T(8,128)}, f32[128,512]{1,0:T(8,128)}, f32[128,512]{1,0:T(8,128)}, /*index=5*/f32[128,512]{1,0:T(8,128)}) async-done(((f32[128,1024]{1,0:T(8,128)}, f32[128,512]{1,0:T(8,128)}, f32[128,512]{1,0:T(8,128)}, f32[128,512]{1,0:T(8,128)}, f32[128,512]{1,0:T(8,128)}, /*index=5*/f32[128,512]{1,0:T(8,128)}), ...) | async-done | bytes 1835024 | tf_op jit(solution)/shard_map/psum | solution.py:45
  56.0 89.8 %all-reduce.33 = (bf16[128,1024]{1,0:T(8,128)(2,1)S(1)}, bf16[128,512]{1,0:T(8,128)(2,1)S(1)}) all-reduce(f32[128,1024]{1,0:T(8,128)S(1)} %copy-done.14, f32[128,512]{1,0:T(8,128)} %get-tuple-element.76), channel_id=1, replica_groups=mesh['rows'=16,'cols'=2] {'rows'}, use_global_device_ids=true, to_apply=%region_6.9 | all-reduce | flops 196608 | bytes 1179648 | tf_op jit(solution)/shard_map/psum | solution.py:44
  146.6 31.8 %all-reduce.24.cloned.1.call-done = (f32[128,512]{1,0:T(8,128)}, f32[128,512]{1,0:T(8,128)}, f32[128,512]{1,0:T(8,128)}, f32[128,512]{1,0:T(8,128)}) async-done(((f32[128,512]{1,0:T(8,128)}, f32[128,512]{1,0:T(8,128)}, f32[128,512]{1,0:T(8,128)}, f32[128,512]{1,0:T(8,128)}), (f32[128,512]{1,0:T(8,128)}, f32[128,512]{1,0:T(8,128)}, f32[128,512]{1,0:T(8,128)}, ...) | async-done | bytes 1048592 | tf_op jit(solution)/shard_map/psum | solution.py:44
  178.3 1.1 multiply_reduce_fusion.4
  179.4 1.2 fusion.43
  181.0 11.7 %cholesky.74 = f32[128,128]{1,0:T(8,128)S(1)} custom-call(f32[128,128]{1,0:T(8,128)S(1)} %fusion.93), custom_call_target="Cholesky" | custom-call | tf_op jit(solution)/shard_map/jit(cholesky)/cholesky | solution.py:73
  194.0 9.8 %custom-call.8 = f32[1,128,128]{1,2,0:T(8,128)S(1)} custom-call(f32[1,128,128]{2,1,0:T(8,128)S(1)} %fusion.82), custom_call_target="InvertDiagBlocksLowerTriangular" | custom-call | tf_op jit(solution)/shard_map/triangular_solve/custom-call.0 | solution.py:74
  204.9 1.1 fusion.33
  206.0 1.0 gather_fusion.5
  207.9 1.1 gather_fusion.7
  210.7 15.4 %all-reduce.30.cloned.1.call-done = (f32[128,1024]{1,0:T(8,128)}, f32[128,512]{1,0:T(8,128)}) async-done(((f32[128,1024]{1,0:T(8,128)}, f32[128,512]{1,0:T(8,128)}), (f32[128,1024]{1,0:T(8,128)}, f32[128,512]{1,0:T(8,128)})) %all-reduce.30.cloned.1.call-update) | async-done | bytes 786448 | tf_op jit(solution)/shard_map/psum | solution.py:45
  226.1 87.2 %all-reduce.34 = (bf16[128,1024]{1,0:T(8,128)(2,1)S(1)}, bf16[128,512]{1,0:T(8,128)(2,1)S(1)}) all-reduce(f32[128,1024]{1,0:T(8,128)} %get-tuple-element.73, f32[128,512]{1,0:T(8,128)} %get-tuple-element.74), channel_id=1, replica_groups=mesh['rows'=16,'cols'=2] {'rows'}, use_global_device_ids=true, to_apply=%region_16.21 | all-reduce | flops 196608 | bytes 1179648 | tf_op jit(solution)/shard_map/psum | solution.py:44
  313.4 1.2 fusion.17
  315.7 1.6 copy.35
  317.3 1.5 fusion.91
  318.8 13.2 %cholesky.85 = f32[128,128]{1,0:T(8,128)} custom-call(f32[128,128]{1,0:T(8,128)} %fusion.91), custom_call_target="Cholesky" | custom-call | tf_op jit(solution)/shard_map/jit(cholesky)/cholesky | solution.py:73
  333.5 2.1 fusion.83
  335.6 11.3 %custom-call.9 = f32[1,128,128]{1,2,0:T(8,128)} custom-call(f32[1,128,128]{2,1,0:T(8,128)} %fusion.83), custom_call_target="InvertDiagBlocksLowerTriangular" | custom-call | tf_op jit(solution)/shard_map/triangular_solve/custom-call.0 | solution.py:74
  346.9 1.1 fusion.69
  348.7 1.0 fusion.35
  351.6 1.1 gather_fusion.10
  354.4 12.6 %all-reduce.28.cloned.1.call-done = (f32[128,1024]{1,0:T(8,128)}, f32[128,512]{1,0:T(8,128)}) async-done(((f32[128,1024]{1,0:T(8,128)}, f32[128,512]{1,0:T(8,128)}), (f32[128,1024]{1,0:T(8,128)}, f32[128,512]{1,0:T(8,128)})) %all-reduce.28.cloned.1.call-update) | async-done | bytes 786448 | tf_op jit(solution)/shard_map/psum | solution.py:45
  367.0 86.8 %all-reduce.35 = (bf16[128,1024]{1,0:T(8,128)(2,1)S(1)}, bf16[128,512]{1,0:T(8,128)(2,1)}) all-reduce(f32[128,1024]{1,0:T(8,128)} %get-tuple-element.71, f32[128,512]{1,0:T(8,128)} %get-tuple-element.72), channel_id=1, replica_groups=mesh['rows'=16,'cols'=2] {'rows'}, use_global_device_ids=true, to_apply=%region_24.29 | all-reduce | flops 196608 | bytes 1179648 | tf_op jit(solution)/shard_map/psum | solution.py:44
  455.8 12.5 %cholesky.96 = f32[128,128]{1,0:T(8,128)S(1)} custom-call(f32[128,128]{1,0:T(8,128)} %fusion.89), custom_call_target="Cholesky" | custom-call | tf_op jit(solution)/shard_map/jit(cholesky)/cholesky | solution.py:73
  469.7 9.8 %custom-call.10 = f32[1,128,128]{1,2,0:T(8,128)S(1)} custom-call(f32[1,128,128]{2,1,0:T(8,128)S(1)} %fusion.84), custom_call_target="InvertDiagBlocksLowerTriangular" | custom-call | tf_op jit(solution)/shard_map/triangular_solve/custom-call.0 | solution.py:74
  480.5 1.2 fusion.37
  481.7 1.1 gather_fusion.11
  483.8 15.3 %all-reduce.26.cloned.1.call-done = (f32[128,1024]{1,0:T(8,128)}, f32[128,512]{1,0:T(8,128)}) async-done(((f32[128,1024]{1,0:T(8,128)}, f32[128,512]{1,0:T(8,128)}), (f32[128,1024]{1,0:T(8,128)}, f32[128,512]{1,0:T(8,128)})) %all-reduce.26.cloned.1.call-update) | async-done | bytes 786448 | tf_op jit(solution)/shard_map/psum | solution.py:45
  499.1 86.8 %all-reduce.36 = (bf16[128,1024]{1,0:T(8,128)(2,1)S(1)}, bf16[128,512]{1,0:T(8,128)(2,1)}) all-reduce(f32[128,1024]{1,0:T(8,128)} %get-tuple-element.69, f32[128,512]{1,0:T(8,128)} %get-tuple-element.70), channel_id=1, replica_groups=mesh['rows'=16,'cols'=2] {'rows'}, use_global_device_ids=true, to_apply=%region_31.36 | all-reduce | flops 196608 | bytes 1179648 | tf_op jit(solution)/shard_map/psum | solution.py:44
  587.2 11.7 %cholesky.107 = f32[128,128]{1,0:T(8,128)S(1)} custom-call(f32[128,128]{1,0:T(8,128)S(1)} %fusion.87), custom_call_target="Cholesky" | custom-call | tf_op jit(solution)/shard_map/jit(cholesky)/cholesky | solution.py:73
  600.3 9.8 %custom-call.11 = f32[1,128,128]{1,2,0:T(8,128)S(1)} custom-call(f32[1,128,128]{2,1,0:T(8,128)S(1)} %fusion.85), custom_call_target="InvertDiagBlocksLowerTriangular" | custom-call | tf_op jit(solution)/shard_map/triangular_solve/custom-call.0 | solution.py:74
  612.5 5.8 all-gather.2.cloned.1.call-done
  618.4 1.1 constant_dynamic-slice_fusion
  619.5 3.5 fusion.63
  623.1 1.7 fusion.62
  624.8 119.0 %all-reduce.22.cloned.1.call-done = (f32[512,512]{1,0:T(8,128)}, f32[512,256]{1,0:T(8,128)}) async-done(((f32[512,512]{1,0:T(8,128)}, f32[512,256]{1,0:T(8,128)}), (f32[512,512]{1,0:T(8,128)}, f32[512,256]{1,0:T(8,128)})) %all-reduce.22.cloned.1.call-update) | async-done | bytes 1572880 | tf_op jit(solution)/shard_map/psum | solution.py:84
  743.7 1.5 dynamic-slice_multiply_fusion
  745.2 1.4 dynamic-slice_multiply_fusion.1
  (140 shorter events, 31.8 us)
Async XLA Ops:
  7.2 3.6 copy-start.20
  7.2 3.6 copy-start.18
  7.2 5.4 all-to-all-start
  11.4 4.9 copy-start.25
  12.5 10.2 %all-to-all-start.1 = ((bf16[2,640,512]{2,1,0:T(8,128)(2,1)}), bf16[2,640,512]{2,1,0:T(8,128)(2,1)S(1)}, u32[]{:S(2)}, u32[]{:S(2)}) async-start(bf16[2,640,512]{2,1,0:T(8,128)(2,1)} %bitcast.251), calls=%async_computation.1 | async-start | bytes 2621440 | tf_op jit(solution)/shard_map/all_to_all | solution.py:24
  16.2 38.8 %all-reduce.32.cloned.1.call-start = ((), (), s32[]{:S(2)}) async-start(), calls=%async_computation.8 | async-start | bytes 3670016 | tf_op jit(solution)/shard_map/psum | solution.py:45
  16.3 0.9 copy-start.24
  20.4 0.9 copy-start.23
  21.9 3.4 copy-start.22
  22.8 1.1 copy-start.1
  25.3 2.7 copy-start.13
  30.8 1.3 copy-start.19
  30.8 1.3 copy-start.21
  30.8 1.3 copy-start.16
  30.8 1.3 copy-start.17
  30.8 147.5 %all-reduce.24.cloned.1.call-start = ((), (), s32[]{:S(2)}) async-start(), calls=%async_computation.4 | async-start | bytes 2097152 | tf_op jit(solution)/shard_map/psum | solution.py:44
  54.9 1.0 copy-start.14
  55.0 171.1 %all-reduce.30.cloned.1.call-start = ((), (), s32[]{:S(2)}) async-start(), calls=%async_computation.7 | async-start | bytes 1572864 | tf_op jit(solution)/shard_map/psum | solution.py:45
  178.3 25.9 %copy-start.5 = (f32[128,512]{1,0:T(8,128)S(1)}, f32[128,512]{1,0:T(8,128)}, u32[]{:S(2)}) copy-start(f32[128,512]{1,0:T(8,128)} %get-tuple-element.65) | copy-start | bytes 786436
  207.8 2.7 copy-start.4
  207.8 159.2 %all-reduce.28.cloned.1.call-start = ((), (), s32[]{:S(2)}) async-start(), calls=%async_computation.6 | async-start | bytes 1572864 | tf_op jit(solution)/shard_map/psum | solution.py:45
  314.7 33.3 %copy-start.7 = (f32[640,128]{1,0:T(8,128)S(1)}, f32[640,128]{1,0:T(8,128)}, u32[]{:S(2)}) copy-start(f32[640,128]{1,0:T(8,128)} %fusion.17) | copy-start | bytes 983044
  351.5 2.8 copy-start.3
  351.5 147.6 %all-reduce.26.cloned.1.call-start = ((), (), s32[]{:S(2)}) async-start(), calls=%async_computation.5 | async-start | bytes 1572864 | tf_op jit(solution)/shard_map/psum | solution.py:45
  453.8 1.0 copy-start.10
  454.8 25.3 %copy-start.11 = (bf16[128,512]{1,0:T(8,128)(2,1)S(1)}, bf16[128,512]{1,0:T(8,128)(2,1)}, u32[]{:S(2)}) copy-start(bf16[128,512]{1,0:T(8,128)(2,1)} %get-tuple-element.58) | copy-start | bytes 393220
  481.7 2.0 copy-start.2
  483.6 134.7 %all-gather.2.cloned.1.call-start = ((), (), s32[]{:S(2)}) async-start(), calls=%async_computation.2 | async-start | bytes 1966080 | tf_op jit(solution)/shard_map/all_gather | solution.py:77
  586.0 1.0 copy-start.8
  586.9 23.8 %copy-start.9 = (bf16[128,512]{1,0:T(8,128)(2,1)S(1)}, bf16[128,512]{1,0:T(8,128)(2,1)}, u32[]{:S(2)}) copy-start(bf16[128,512]{1,0:T(8,128)(2,1)} %get-tuple-element.56) | copy-start | bytes 393220
  611.1 8.4 %copy-start.6 = (bf16[1280,512]{1,0:T(8,128)(2,1)S(1)}, bf16[1280,512]{1,0:T(8,128)(2,1)}, u32[]{:S(2)}) copy-start(bf16[1280,512]{1,0:T(8,128)(2,1)} %param.21) | copy-start | bytes 3932164
  611.1 8.4 %copy-start.26 = (f32[1280]{0:T(1024)S(1)}, f32[1280]{0:T(1024)}, u32[]{:S(2)}) copy-start(f32[1280]{0:T(1024)} %param.22) | copy-start | bytes 15364
  611.6 0.8 copy-start
  612.5 131.3 %all-reduce.22.cloned.1.call-start = ((), (), s32[]{:S(2)}) async-start(), calls=%async_computation.3 | async-start | bytes 3145728 | tf_op jit(solution)/shard_map/psum | solution.py:84
  619.5 3.6 copy-start.12
  619.5 3.6 copy-start.15
Sparse Core Ops, SparseCore 0:
  30.9 24.0 all-reduce.31
  60.7 117.6 all-reduce.23
  207.9 18.0 all-reduce.29
  351.7 15.3 all-reduce.27
  483.7 15.3 all-reduce.25
  612.6 5.7 all-gather.1
  624.9 118.8 all-reduce.21
